TPU v7x, 32 devices: a whole 2x2x4 slice. The times are simulated.
32 devices in a mesh: dom: 8 (over z, x), cls: 4 (over y, core).
Axes of the slice: x: 2, y: 2, z: 4, core: 2. Of those that a mesh axis runs over, the one named last changes fastest.
Arguments:
- spectra: bfloat16 [512, 128, 512], P(('dom', 'cls')), may hold values from -6 to 6
- ctf: bfloat16 [512, 128], P(('dom', 'cls')), may hold values from -1 to 1
- noise_power: float32 [128], replicated, may hold values from 0.5 to 8
- references: bfloat16 [48, 32, 512], P('cls'), may hold values from -3 to 3
- owner: int32 [512, 1], P(('dom', 'cls')), may hold values from 0 to 3; in each aligned block of 16 rows (0 to 15, 16 to 31, ...) at most 8 rows name the same one
- sub_class: int32 [512], P(('dom', 'cls')), may hold values from 0 to 11
- rotation: int32 [512], P(('dom', 'cls')), may hold values from 0 to 511
Outputs:
- new_refs: float32 [48, 128, 512], P('cls', 'dom')
- log_evidence: float32 [512], P(('dom', 'cls'))
Inputs may be any that keep to these rules, and one draw needn't show every extreme that they name: Among the 16 particles of one device, at most 8 have the same owner, a bound that some block reaches of them.
All inputs are finite; a program needn't handle non-finite values.
Results may differ from a plain program's by a relative error of at most 0.00067.
Values may be sent and summed in bfloat16 or wider, within the bound.
No kernel may reach another device: no remote copies, remote signals or barrier semaphores. Data moves between devices by JAX's collectives and lax.ppermute only.
A program may use at most 128 MiB of HBM per device.

v0:
```python
import math
import jax
import jax.numpy as jnp
from jax import lax
from jax.sharding import PartitionSpec as P


def rotation_table(half, turns_all):
    freq = jnp.arange(half, dtype=jnp.int32)
    steps = jnp.arange(turns_all, dtype=jnp.int32)
    turns = freq[:, None] * steps[None, :] % turns_all
    angle = turns.astype(jnp.float32) * (2.0 * math.pi / turns_all)
    return jnp.concatenate([jnp.cos(angle), -jnp.sin(angle)], axis=0).astype(jnp.bfloat16)


def paired_rows(weighted):
    half = weighted.shape[2] // 2
    direct = jnp.concatenate([weighted[..., :half], weighted[..., half:]], axis=1)
    swapped = jnp.concatenate([weighted[..., half:], -weighted[..., :half]], axis=1)
    return jnp.concatenate([direct, swapped], axis=0)


def piece_scores(paired, cw_low, piece, table):
    half = piece.shape[2] // 2
    count = cw_low.shape[0]
    kinds = piece.shape[0]
    stacked = jnp.concatenate([piece[..., :half], piece[..., half:]], axis=1)
    both = jnp.einsum("nqf,kqf->nkf", paired, stacked, preferred_element_type=jnp.float32)
    cross = jnp.concatenate([both[:count], both[count:]], axis=-1).astype(jnp.bfloat16)
    corr = jnp.dot(
        cross.reshape(count * kinds, 2 * half), table, preferred_element_type=jnp.float32
    )
    corr = corr.reshape(count, kinds, table.shape[1])
    ynorm = jnp.sum(jnp.square(piece.astype(jnp.float32)), axis=-1)
    energy = jnp.dot(cw_low, ynorm.T, precision=lax.Precision.HIGHEST)
    return corr - 0.5 * energy[:, :, None]


def fold_evidence(carry, score):
    top, total = carry
    new_top = jnp.max(score, axis=(1, 2))
    total = total * jnp.exp(top - new_top) + jnp.sum(
        jnp.exp(score - new_top[:, None, None]), axis=(1, 2)
    )
    return (new_top, total)


def align_slots(images, ctf_recv, turn_index, noise, half, turns_all):
    cfl = ctf_recv.astype(jnp.float32)
    wr = cfl / noise
    turns = jnp.arange(half, dtype=jnp.int32) * turn_index[..., None] % turns_all
    angle = turns.astype(jnp.float32) * (2.0 * math.pi / turns_all)
    cosv = jnp.cos(angle)[..., None, :]
    sinv = jnp.sin(angle)[..., None, :]
    values = images.astype(jnp.float32)
    x_re = values[..., :half]
    x_im = values[..., half:]
    a_re = wr[..., None] * (x_re * cosv - x_im * sinv)
    a_im = wr[..., None] * (x_re * sinv + x_im * cosv)
    return (jnp.concatenate([a_re, a_im], axis=-1), cfl * wr)


def per_device(spectra, ctf, noise_power, references, owner, sub_class, rotation):
    count = spectra.shape[0]
    cycles = spectra.shape[1]
    half = spectra.shape[2] // 2
    low_cycles = references.shape[1]
    k_local = references.shape[0]
    turns_all = 2 * half
    shards = lax.axis_size("cls")
    table = rotation_table(half, turns_all)
    weight = ctf.astype(jnp.float32) / noise_power[None, :]
    weighted = (
        weight[:, :low_cycles, None] * spectra[:, :low_cycles, :].astype(jnp.float32)
    ).astype(jnp.bfloat16)
    empty = (jnp.full((count,), -jnp.inf, jnp.float32), jnp.zeros((count,), jnp.float32))
    paired = paired_rows(weighted)
    cw_low = ctf[:, :low_cycles].astype(jnp.float32) * weight[:, :low_cycles]
    top, total = fold_evidence(
        empty,
        piece_scores(paired, cw_low, lax.all_gather(references, "cls", axis=0, tiled=True), table),
    )
    log_evidence = top + jnp.log(total)
    capacity = max(2, 2 * count // shards)
    slots = shards * capacity
    dest = owner[:, 0]
    hit = (dest[:, None] == jnp.arange(shards, dtype=jnp.int32)[None, :]).astype(jnp.int32)
    rank = jnp.sum((jnp.cumsum(hit, axis=0) - hit) * hit, axis=1)
    target = dest * capacity + rank
    place = jnp.arange(slots, dtype=jnp.int32)[:, None] == target[None, :]
    place_half = place.astype(jnp.bfloat16)
    send_img = jnp.dot(
        place_half, spectra.reshape(count, cycles * 2 * half), preferred_element_type=jnp.float32
    )
    send_img = send_img.astype(jnp.bfloat16).reshape(shards, capacity, cycles, 2 * half)
    send_ctf = (
        jnp.dot(place_half, ctf, preferred_element_type=jnp.float32)
        .astype(jnp.bfloat16)
        .reshape(shards, capacity, cycles)
    )
    placed = place.astype(jnp.int32)
    send_meta = jnp.stack(
        [jnp.sum(placed * rotation[None, :], axis=1), jnp.sum(placed * sub_class[None, :], axis=1)],
        axis=-1,
    )
    send_meta = send_meta.reshape(shards, capacity, 2)
    images = lax.all_to_all(send_img, "cls", split_axis=0, concat_axis=0, tiled=True)
    ctf_recv = lax.all_to_all(send_ctf, "cls", split_axis=0, concat_axis=0, tiled=True)
    meta = lax.all_to_all(send_meta, "cls", split_axis=0, concat_axis=0, tiled=True)
    aligned_part, cw_part = align_slots(
        images, ctf_recv, meta[:, :, 0], noise_power, half, turns_all
    )
    local = meta[:, :, 1]
    member = (
        local.reshape(slots)[:, None] == jnp.arange(k_local, dtype=jnp.int32)[None, :]
    ).astype(jnp.float32)
    numer = jnp.dot(
        member.T, aligned_part.reshape(slots, cycles * 2 * half), precision=lax.Precision.HIGHEST
    )
    numer = numer.reshape(k_local, cycles, 2 * half)
    denom = jnp.dot(member.T, cw_part.reshape(slots, cycles), precision=lax.Precision.HIGHEST)
    numer_part, denom_part = (
        lax.psum_scatter(numer, "dom", scatter_dimension=1, tiled=True),
        lax.psum_scatter(denom, "dom", scatter_dimension=1, tiled=True),
    )
    new_refs = numer_part / (denom_part + 1.0)[:, :, None]
    return (new_refs, log_evidence)


def solution(mesh):
    return jax.shard_map(
        per_device,
        mesh=mesh,
        in_specs=(
            P(("dom", "cls"), None, None),
            P(("dom", "cls"), None),
            P(),
            P("cls", None, None),
            P(("dom", "cls"), None),
            P(("dom", "cls")),
            P(("dom", "cls")),
        ),
        out_specs=(P("cls", "dom", None), P(("dom", "cls"))),
        check_vma=False,
    )
```

profile of v0, /device:TPU:0, one launch (start us, length us, event | category | flops | bytes accessed | tf_op | source)
XLA Modules:
  0.0 201.9 jit_solution(9103172688339019743)
XLA Ops:
  11.8 4.3 %all-to-all-start = ((s32[4,8,2]{1,2,0:T(2,128)}), s32[4,8,2]{1,2,0:T(2,128)S(1)}, u32[]{:S(2)}, u32[]{:S(2)}) async-start(s32[4,8,2]{1,2,0:T(2,128)} %copy.32), calls=%async_computation | async-start | bytes 8192 | tf_op jit(solution)/shard_map/all_to_all | solution.py:109
  16.1 1.5 fusion.18
  17.6 2.8 %copy.48 = bf16[2,8,128,512]{3,1,2,0:T(8,128)(2,1)S(1)} copy(bf16[2,8,128,512]{3,2,1,0:T(8,128)(2,1)} %bitcast.40) | data formatting | bytes 4194304
  20.4 3.3 %all-to-all-start.1 = ((bf16[4,8,128]{2,1,0:T(8,128)(2,1)}), bf16[4,8,128]{2,1,0:T(8,128)(2,1)S(1)}, u32[]{:S(2)}, u32[]{:S(2)}) async-start(bf16[4,8,128]{2,1,0:T(8,128)(2,1)} %fusion.18), calls=%async_computation.1 | async-start | bytes 16384 | tf_op jit(solution)/shard_map/all_to_all | solution.py:108
  23.7 3.3 %convolution_convert_fusion = bf16[32,65536]{1,0:T(8,128)(2,1)} fusion(bf16[16,65536]{1,0:T(8,128)(2,1)S(1)} %bitcast.39, s32[16]{0:T(128)S(1)} %multiply_add_fusion), kind=kOutput, calls=%fused_computation | convolution fusion | flops 69206528 | bytes 6291520 | tf_op jit(solution)/shard_map/dot_general | solution.py:92
  27.5 5.0 %all-to-all-start.2 = ((bf16[4,8,128,512]{3,1,2,0:T(8,128)(2,1)}), bf16[4,8,128,512]{3,1,2,0:T(8,128)(2,1)}, u32[]{:S(2)}, u32[]{:S(2)}) async-start(bf16[4,8,128,512]{3,1,2,0:T(8,128)(2,1)} %bitcast.38), calls=%async_computation.2 | async-start | bytes 8388608 | tf_op jit(solution)/shard_map/all_to_all | solution.py:107
  34.5 54.6 %all-to-all-done.2 = bf16[4,8,128,512]{3,1,2,0:T(8,128)(2,1)} async-done(((bf16[4,8,128,512]{3,1,2,0:T(8,128)(2,1)}), bf16[4,8,128,512]{3,1,2,0:T(8,128)(2,1)}, u32[]{:S(2)}, u32[]{:S(2)}) %all-to-all-start.2) | async-done | bytes 4194336 | tf_op jit(solution)/shard_map/all_to_all | solution.py:107
  89.1 3.4 %convert_element_type.56 = f32[4,8,128,512]{3,1,2,0:T(8,128)S(1)} convert(bf16[4,8,128,512]{3,1,2,0:T(8,128)(2,1)} %all-to-all-done.2) | non-fusion elementwise | flops 2097152 | bytes 12582912 | tf_op jit(solution)/shard_map/convert_element_type | solution.py:55
  92.5 1.4 subtract_multiply_fusion
  93.9 5.3 %fusion = f32[12,128,512]{2,0,1:T(8,128)} fusion(s32[32]{0:T(128)S(1)} %eq.51, f32[4,8,128,256]{3,1,2,0:T(8,128)S(1)} %get-tuple-element.13, f32[4,8,128,256]{3,1,2,0:T(8,128)S(1)} %get-tuple-element.12), kind=kOutput, calls=%fused_computation.1 | convolution fusion | flops 304087424 | bytes 11534464 | tf_op jit(solution)/shard_map/dot_general | solution.py:117
  99.3 1.1 slice.51
  100.4 2.0 copy.46
  102.3 2.9 %negate_convert_fusion = (bf16[256,512]{1,0:T(8,128)(2,1)}, bf16[256,512]{1,0:T(8,128)(2,1)}) fusion(), kind=kLoop, calls=%fused_computation.39 | loop fusion | flops 2228224 | bytes 524288 | tf_op jit(solution)/shard_map/convert.1
  105.7 1.9 fusion.51
  108.5 2.6 %fusion.52 = (bf16[48,32,256]{2,1,0:T(8,128)(2,1)}, bf16[48,32,256]{2,1,0:T(8,128)(2,1)}) fusion(bf16[48,32,512]{2,1,0:T(8,128)(2,1)} %all-gather.2.cloned.1.call-done), kind=kLoop, calls=%fused_computation.84 | loop fusion | bytes 3145728 | tf_op jit(solution)/shard_map/slice | solution.py:27
  111.1 3.8 %copy.45 = bf16[48,32,256]{1,0,2:T(8,128)(2,1)S(1)} copy(bf16[48,32,256]{2,1,0:T(8,128)(2,1)} %get-tuple-element.20) | data formatting | bytes 1572864
  114.9 4.9 %copy.44 = bf16[48,32,256]{1,0,2:T(8,128)(2,1)} copy(bf16[48,32,256]{2,1,0:T(8,128)(2,1)} %get-tuple-element.19) | data formatting | bytes 1572864
  119.9 6.0 %convert_bitcast_fusion = bf16[32,48,256]{1,0,2:T(8,128)(2,1)S(1)} fusion(bf16[16,32,256]{1,0,2:T(8,128)(2,1)} %get-tuple-element.17, bf16[16,32,256]{1,0,2:T(8,128)(2,1)} %get-tuple-element.18, bf16[16,32,256]{1,0,2:T(8,128)(2,1)} %get-tuple-element.16, bf16[48,32,256]{1,0,2:T(8,128)(2,1)S(1)} %copy.45, bf16[48,32,256]{1,0,2:T(8,128)(2,1)} %copy.44), kind=kOutput, calls=%fused_computation.20 | convolution fusion | flops 58064896 | bytes 3145728 | tf_op jit(solution)/shard_map/nqf,kqf->nkf/dot_general | solution.py:28
  125.9 1.3 fusion.50
  127.3 2.0 copy.40
  130.6 1.7 fusion.53
  133.3 59.0 %reduce-scatter.5.cloned.1.call-done = f32[12,16,512]{2,0,1:T(8,128)} async-done(((f32[12,128,512]{2,0,1:T(8,128)}), f32[12,16,512]{2,0,1:T(8,128)}) %reduce-scatter.5.cloned.1.call-update) | async-done | bytes 393232 | tf_op jit(solution)/shard_map/reduce_scatter | solution.py:123
  192.3 1.1 broadcast_divide_fusion
  193.5 1.0 copy.41
  (41 shorter events, 9.9 us)
Async XLA Ops:
  11.8 8.6 %all-to-all-start = ((s32[4,8,2]{1,2,0:T(2,128)}), s32[4,8,2]{1,2,0:T(2,128)S(1)}, u32[]{:S(2)}, u32[]{:S(2)}) async-start(s32[4,8,2]{1,2,0:T(2,128)} %copy.32), calls=%async_computation | async-start | bytes 8192 | tf_op jit(solution)/shard_map/all_to_all | solution.py:109
  20.4 7.1 %all-to-all-start.1 = ((bf16[4,8,128]{2,1,0:T(8,128)(2,1)}), bf16[4,8,128]{2,1,0:T(8,128)(2,1)S(1)}, u32[]{:S(2)}, u32[]{:S(2)}) async-start(bf16[4,8,128]{2,1,0:T(8,128)(2,1)} %fusion.18), calls=%async_computation.1 | async-start | bytes 16384 | tf_op jit(solution)/shard_map/all_to_all | solution.py:108
  27.5 5.2 %copy-start.2 = (f32[128]{0:T(128)S(1)}, f32[128]{0:T(128)}, u32[]{:S(2)}) copy-start(f32[128]{0:T(128)} %param.9) | copy-start | bytes 1540
  27.5 61.6 %all-to-all-start.2 = ((bf16[4,8,128,512]{3,1,2,0:T(8,128)(2,1)}), bf16[4,8,128,512]{3,1,2,0:T(8,128)(2,1)}, u32[]{:S(2)}, u32[]{:S(2)}) async-start(bf16[4,8,128,512]{3,1,2,0:T(8,128)(2,1)} %bitcast.38), calls=%async_computation.2 | async-start | bytes 8388608 | tf_op jit(solution)/shard_map/all_to_all | solution.py:107
  32.5 75.1 %reduce-scatter.7.cloned.1.call-start = ((), (), s32[]{:S(2)}) async-start(), calls=%async_computation.7 | async-start | bytes 73728
  33.6 74.9 %all-gather.2.cloned.1.call-start = ((), (), s32[]{:S(2)}) async-start(), calls=%async_computation.6 | async-start | bytes 1966080 | tf_op jit(solution)/shard_map/all_gather | solution.py:81
  34.1 158.2 %reduce-scatter.5.cloned.1.call-start = ((), (), s32[]{:S(2)}) async-start(), calls=%async_computation.5 | async-start | bytes 4718592 | tf_op jit(solution)/shard_map/reduce_scatter | solution.py:123
  99.2 6.0 %copy-start.1 = (bf16[16,128]{1,0:T(8,128)(2,1)S(1)}, bf16[16,128]{1,0:T(8,128)(2,1)}, u32[]{:S(2)}) copy-start(bf16[16,128]{1,0:T(8,128)(2,1)} %param.8) | copy-start | bytes 12292
  125.9 4.2 %copy-start = (bf16[48,32,512]{2,1,0:T(8,128)(2,1)S(1)}, bf16[48,32,512]{2,1,0:T(8,128)(2,1)}, u32[]{:S(2)}) copy-start(bf16[48,32,512]{2,1,0:T(8,128)(2,1)} %all-gather.2.cloned.1.call-done) | copy-start | bytes 4718596
Sparse Core Ops, SparseCore 0:
  36.7 64.5 reduce-scatter.6
  104.9 87.3 reduce-scatter.4
Sparse Core Ops, SparseCore 1:
  35.6 30.1 all-gather.1
where the time goes:
time: 203 us; the launch traced here: 202 us
  waiting for transfers between devices  115 us (57%)
  local copies, waits for them, and re-layouts  24.3 us (12%)
  matrix products  19 us (9%)
  other arithmetic  15.7 us (8%)
  between operations  15.6 us (8%)
  starting transfers between devices  12.7 us (6%)
    reduce_scatter x1, waiting for transfers between devices, per_device(): lax.psum_scatter(numer, 'dom', scatter_dimension=1, tiled=True)  59 us
    all_to_all x1, waiting for transfers between devices, per_device(): lax.all_to_all(send_img, 'cls', split_axis=0, concat_axis=0, tiled=True)  54.6 us
    unnamed x12, local copies, waits for them, and re-layouts  15.3 us
    dot_general x1, matrix products, piece_scores(): jnp.einsum('nqf,kqf->nkf', paired, stacked, preferred_element_type=jnp.fl...  6.05 us
    dot_general x1, matrix products, per_device(): jnp.dot(member.T, aligned_part.reshape(slots, cycles * 2 * half), precisi...  5.33 us
    all_to_all x1, starting transfers between devices, per_device(): lax.all_to_all(send_img, 'cls', split_axis=0, concat_axis=0, tiled=True)  4.99 us
    all_to_all x1, starting transfers between devices, per_device(): lax.all_to_all(send_meta, 'cls', split_axis=0, concat_axis=0, tiled=True)  4.26 us
  transfers between devices with their start and end apart: 6, of which 3 were waited for; matrix products, arithmetic and copies ran while one was open for 26% of the time, Pallas kernels for 0%

commit v1 on v0

--- a/solution.py
+++ b/solution.py
@@ -3,6 +3,22 @@
 import jax.numpy as jnp
 from jax import lax
 from jax.sharding import PartitionSpec as P
+
+
+def pairwise_exchange(x, axis, split, join):
+    ways, here = (lax.axis_size(axis), lax.axis_index(axis))
+    width = x.shape[split] // ways
+    shape = list(x.shape)
+    shape[split] = width
+    height = shape[join]
+    shape[join] = height * ways
+    full = jnp.zeros(shape, x.dtype)
+    for mask in range(ways):
+        part = lax.dynamic_slice_in_dim(x, (here ^ mask) * width, width, axis=split)
+        if mask:
+            part = lax.ppermute(part, axis, [(d, d ^ mask) for d in range(ways)])
+        full = lax.dynamic_update_slice_in_dim(full, part, (here ^ mask) * height, axis=join)
+    return full
 
 
 def rotation_table(half, turns_all):
@@ -104,7 +120,7 @@
         axis=-1,
     )
     send_meta = send_meta.reshape(shards, capacity, 2)
-    images = lax.all_to_all(send_img, "cls", split_axis=0, concat_axis=0, tiled=True)
+    images = pairwise_exchange(send_img, "cls", 0, 0)
     ctf_recv = lax.all_to_all(send_ctf, "cls", split_axis=0, concat_axis=0, tiled=True)
     meta = lax.all_to_all(send_meta, "cls", split_axis=0, concat_axis=0, tiled=True)
     aligned_part, cw_part = align_slots(

time: 203 us -> 206 us (1.015)
  local copies, waits for them, and re-layouts: 24.3 us -> 35.6 us
  waiting for transfers between devices: 115 us -> 109 us
  starting transfers between devices: 12.7 us -> 9.5 us
    all_to_all x1 -> x0, waiting for transfers between devices: 54.6 us -> none  [per_device(): lax.all_to_all(send_img, 'cls', split_axis=0, concat_axis=0, tiled=True)]
    ppermute x0 -> x3, waiting for transfers between devices: none -> 47.7 us  [pairwise_exchange(): part = lax.ppermute(part, axis, [(d, d ^ mask) for d in range(ways)])]
    dynamic_update_slice x0 -> x3, local copies, waits for them, and re-layouts: none -> 6.89 us  [pairwise_exchange(): lax.dynamic_update_slice_in_dim(full, part, (here ^ mask) * height, axis=...]
    all_to_all x1 -> x0, starting transfers between devices: 4.99 us -> none  [per_device(): lax.all_to_all(send_img, 'cls', split_axis=0, concat_axis=0, tiled=True)]
    reduce_scatter x1, waiting for transfers between devices: 59 us -> 54.5 us  [per_device(): lax.psum_scatter(numer, 'dom', scatter_dimension=1, tiled=True)]
    unnamed x12 -> x16, local copies, waits for them, and re-layouts: 15.3 us -> 19.1 us
    all_to_all x1, waiting for transfers between devices: 0.49 us -> 3.62 us  [per_device(): lax.all_to_all(send_ctf, 'cls', split_axis=0, concat_axis=0, tiled=True)]
    all_to_all x1, waiting for transfers between devices: 0.01 us -> 2.25 us  [per_device(): lax.all_to_all(send_meta, 'cls', split_axis=0, concat_axis=0, tiled=True)]
  transfers between devices with their start and end apart: 6 -> 8, of which waited for: 3 -> 6; matrix products, arithmetic and copies ran while one was open for 26% -> 29% of each run, Pallas kernels for 0% -> 0%
where the time goes in v1:
time: 206 us; the launch traced here: 205 us
  waiting for transfers between devices  109 us (53%)
  local copies, waits for them, and re-layouts  35.6 us (17%)
  matrix products  19.6 us (10%)
  other arithmetic  15.7 us (8%)
  between operations  15.7 us (8%)
  starting transfers between devices  9.5 us (5%)
    reduce_scatter x1, waiting for transfers between devices, per_device(): lax.psum_scatter(numer, 'dom', scatter_dimension=1, tiled=True)  54.5 us
    ppermute x3, waiting for transfers between devices, pairwise_exchange(): part = lax.ppermute(part, axis, [(d, d ^ mask) for d in range(ways)])  47.7 us
    unnamed x16, local copies, waits for them, and re-layouts  19.1 us
    dynamic_update_slice x3, local copies, waits for them, and re-layouts, pairwise_exchange(): lax.dynamic_update_slice_in_dim(full, part, (here ^ mask) * height, axis=...  6.89 us
    dot_general x1, matrix products, piece_scores(): jnp.einsum('nqf,kqf->nkf', paired, stacked, preferred_element_type=jnp.fl...  6.06 us
    dot_general x1, matrix products, per_device(): jnp.dot(member.T, aligned_part.reshape(slots, cycles * 2 * half), precisi...  5.33 us
    all_to_all x1, starting transfers between devices, per_device(): lax.all_to_all(send_meta, 'cls', split_axis=0, concat_axis=0, tiled=True)  4.26 us
  transfers between devices with their start and end apart: 8, of which 6 were waited for; matrix products, arithmetic and copies ran while one was open for 29% of the time, Pallas kernels for 0%

profile of v1, /device:TPU:0, one launch (start us, length us, event | category | flops | bytes accessed | tf_op | source)
XLA Modules:
  0.0 204.8 jit_solution(10233335847039998075)
XLA Ops:
  11.8 4.3 %all-to-all-start = ((s32[4,8,2]{1,2,0:T(2,128)}), s32[4,8,2]{1,2,0:T(2,128)S(1)}, u32[]{:S(2)}, u32[]{:S(2)}) async-start(s32[4,8,2]{1,2,0:T(2,128)} %copy.32), calls=%async_computation | async-start | bytes 8192 | tf_op jit(solution)/shard_map/all_to_all | solution.py:125
  17.6 2.2 %all-to-all-done = s32[4,8,2]{1,2,0:T(2,128)S(1)} async-done(((s32[4,8,2]{1,2,0:T(2,128)}), s32[4,8,2]{1,2,0:T(2,128)S(1)}, u32[]{:S(2)}, u32[]{:S(2)}) %all-to-all-start) | async-done | bytes 288 | tf_op jit(solution)/shard_map/all_to_all | solution.py:125
  19.9 3.2 %all-to-all-start.1 = ((bf16[4,8,128]{2,1,0:T(8,128)(2,1)}), bf16[4,8,128]{2,1,0:T(8,128)(2,1)S(1)}, u32[]{:S(2)}, u32[]{:S(2)}) async-start(bf16[4,8,128]{2,1,0:T(8,128)(2,1)} %fusion.18), calls=%async_computation.1 | async-start | bytes 16384 | tf_op jit(solution)/shard_map/all_to_all | solution.py:124
  23.3 3.6 %all-to-all-done.1 = bf16[4,8,128]{2,1,0:T(8,128)(2,1)S(1)} async-done(((bf16[4,8,128]{2,1,0:T(8,128)(2,1)}), bf16[4,8,128]{2,1,0:T(8,128)(2,1)S(1)}, u32[]{:S(2)}, u32[]{:S(2)}) %all-to-all-start.1) | async-done | bytes 8224 | tf_op jit(solution)/shard_map/all_to_all | solution.py:124
  29.1 2.8 %copy.48 = bf16[2,8,128,512]{3,1,2,0:T(8,128)(2,1)S(1)} copy(bf16[2,8,128,512]{3,2,1,0:T(8,128)(2,1)} %bitcast.40) | data formatting | bytes 4194304
  31.9 3.3 %convolution_convert_fusion = bf16[32,65536]{1,0:T(8,128)(2,1)} fusion(bf16[16,65536]{1,0:T(8,128)(2,1)S(1)} %bitcast.39, s32[16]{0:T(128)S(1)} %multiply_add_fusion), kind=kOutput, calls=%fused_computation | convolution fusion | flops 69206528 | bytes 6291520 | tf_op jit(solution)/shard_map/dot_general | solution.py:108
  35.5 1.9 copy-done
  37.7 1.9 copy-done.1
  42.5 2.3 %constant_dynamic-update-slice_fusion.2 = bf16[4,8,128,512]{3,1,2,0:T(8,128)(2,1)} fusion(bf16[4,8,128,512]{3,1,2,0:T(8,128)(2,1)} %copy-done.1, bf16[1,8,128,512]{3,1,2,0:T(8,128)(2,1)} %collective-permute-done, s32[]{:T(128)S(6)} %select_n.39), kind=kLoop, calls=%fused_computation.82 | loop fusion | bytes 2097156 | tf_op jit(solution)/shard_map/dynamic_update_slice | solution.py:20
  44.8 27.1 %collective-permute-done.1 = bf16[1,8,128,512]{3,1,2,0:T(8,128)(2,1)} collective-permute-done((bf16[1,8,128,512]{3,1,2,0:T(8,128)(2,1)S(1)}, bf16[1,8,128,512]{3,1,2,0:T(8,128)(2,1)}, u32[]{:S(2)}, u32[]{:S(2)}) %collective-permute-start.1) | collective-permute-done | bytes 1048608 | tf_op jit(solution)/shard_map/ppermute | solution.py:19
  71.9 2.3 %constant_dynamic-update-slice_fusion.1 = bf16[4,8,128,512]{3,1,2,0:T(8,128)(2,1)} fusion(bf16[4,8,128,512]{3,1,2,0:T(8,128)(2,1)} %constant_dynamic-update-slice_fusion.2, bf16[1,8,128,512]{3,1,2,0:T(8,128)(2,1)} %collective-permute-done.1, s32[]{:T(128)S(6)} %select_n.40), kind=kLoop, calls=%fused_computation.80 | loop fusion | bytes 2097156 | tf_op jit(solution)/shard_map/dynamic_update_slice | solution.py:20
  74.2 20.0 %collective-permute-done.2 = bf16[1,8,128,512]{3,1,2,0:T(8,128)(2,1)} collective-permute-done((bf16[1,8,128,512]{3,1,2,0:T(8,128)(2,1)S(1)}, bf16[1,8,128,512]{3,1,2,0:T(8,128)(2,1)}, u32[]{:S(2)}, u32[]{:S(2)}) %collective-permute-start.2) | collective-permute-done | bytes 1048608 | tf_op jit(solution)/shard_map/ppermute | solution.py:19
  94.2 2.3 %constant_dynamic-update-slice_fusion = bf16[4,8,128,512]{3,1,2,0:T(8,128)(2,1)} fusion(bf16[4,8,128,512]{3,1,2,0:T(8,128)(2,1)} %constant_dynamic-update-slice_fusion.1, bf16[1,8,128,512]{3,1,2,0:T(8,128)(2,1)} %collective-permute-done.2, s32[]{:T(128)S(6)} %select_n.41), kind=kLoop, calls=%fused_computation.78 | loop fusion | bytes 2097156 | tf_op jit(solution)/shard_map/dynamic_update_slice | solution.py:20
  96.5 3.4 %convert_element_type.56 = f32[4,8,128,512]{3,1,2,0:T(8,128)S(1)} convert(bf16[4,8,128,512]{3,1,2,0:T(8,128)(2,1)} %constant_dynamic-update-slice_fusion) | non-fusion elementwise | flops 2097152 | bytes 12582912 | tf_op jit(solution)/shard_map/convert_element_type | solution.py:71
  101.2 5.3 %fusion = f32[12,128,512]{2,0,1:T(8,128)} fusion(s32[32]{0:T(128)S(1)} %eq.51, f32[4,8,128,256]{3,1,2,0:T(8,128)S(1)} %get-tuple-element.13, f32[4,8,128,256]{3,1,2,0:T(8,128)S(1)} %get-tuple-element.12), kind=kOutput, calls=%fused_computation.1 | convolution fusion | flops 304087424 | bytes 11534464 | tf_op jit(solution)/shard_map/dot_general | solution.py:133
  107.7 2.0 copy.46
  109.7 2.9 %negate_convert_fusion = (bf16[256,512]{1,0:T(8,128)(2,1)}, bf16[256,512]{1,0:T(8,128)(2,1)}) fusion(), kind=kLoop, calls=%fused_computation.40 | loop fusion | flops 2228224 | bytes 524288 | tf_op jit(solution)/shard_map/convert.1
  113.0 1.9 fusion.51
  115.8 2.6 %fusion.52 = (bf16[48,32,256]{2,1,0:T(8,128)(2,1)}, bf16[48,32,256]{2,1,0:T(8,128)(2,1)}) fusion(bf16[48,32,512]{2,1,0:T(8,128)(2,1)} %all-gather.2.cloned.1.call-done), kind=kLoop, calls=%fused_computation.91 | loop fusion | bytes 3145728 | tf_op jit(solution)/shard_map/slice | solution.py:43
  118.4 3.8 %copy.45 = bf16[48,32,256]{1,0,2:T(8,128)(2,1)S(1)} copy(bf16[48,32,256]{2,1,0:T(8,128)(2,1)} %get-tuple-element.24) | data formatting | bytes 1572864
  122.3 4.9 %copy.44 = bf16[48,32,256]{1,0,2:T(8,128)(2,1)} copy(bf16[48,32,256]{2,1,0:T(8,128)(2,1)} %get-tuple-element.23) | data formatting | bytes 1572864
  127.2 6.1 %convert_bitcast_fusion = bf16[32,48,256]{1,0,2:T(8,128)(2,1)S(1)} fusion(bf16[16,32,256]{1,0,2:T(8,128)(2,1)} %get-tuple-element.21, bf16[16,32,256]{1,0,2:T(8,128)(2,1)} %get-tuple-element.22, bf16[16,32,256]{1,0,2:T(8,128)(2,1)} %get-tuple-element.20, bf16[48,32,256]{1,0,2:T(8,128)(2,1)S(1)} %copy.45, bf16[48,32,256]{1,0,2:T(8,128)(2,1)} %copy.44), kind=kOutput, calls=%fused_computation.20 | convolution fusion | flops 58064896 | bytes 3145728 | tf_op jit(solution)/shard_map/nqf,kqf->nkf/dot_general | solution.py:44
  134.6 2.0 copy.40
  140.7 54.5 %reduce-scatter.5.cloned.1.call-done = f32[12,16,512]{2,0,1:T(8,128)} async-done(((f32[12,128,512]{2,0,1:T(8,128)}), f32[12,16,512]{2,0,1:T(8,128)}) %reduce-scatter.5.cloned.1.call-update) | async-done | bytes 393232 | tf_op jit(solution)/shard_map/reduce_scatter | solution.py:139
  (54 shorter events, 22.3 us)
Async XLA Ops:
  11.8 8.1 %all-to-all-start = ((s32[4,8,2]{1,2,0:T(2,128)}), s32[4,8,2]{1,2,0:T(2,128)S(1)}, u32[]{:S(2)}, u32[]{:S(2)}) async-start(s32[4,8,2]{1,2,0:T(2,128)} %copy.32), calls=%async_computation | async-start | bytes 8192 | tf_op jit(solution)/shard_map/all_to_all | solution.py:125
  19.9 7.0 %all-to-all-start.1 = ((bf16[4,8,128]{2,1,0:T(8,128)(2,1)}), bf16[4,8,128]{2,1,0:T(8,128)(2,1)S(1)}, u32[]{:S(2)}, u32[]{:S(2)}) async-start(bf16[4,8,128]{2,1,0:T(8,128)(2,1)} %fusion.18), calls=%async_computation.1 | async-start | bytes 16384 | tf_op jit(solution)/shard_map/all_to_all | solution.py:124
  23.1 91.8 %reduce-scatter.7.cloned.1.call-start = ((), (), s32[]{:S(2)}) async-start(), calls=%async_computation.6 | async-start | bytes 73728
  28.5 87.3 %all-gather.2.cloned.1.call-start = ((), (), s32[]{:S(2)}) async-start(), calls=%async_computation.5 | async-start | bytes 1966080 | tf_op jit(solution)/shard_map/all_gather | solution.py:97
  29.0 166.2 %reduce-scatter.5.cloned.1.call-start = ((), (), s32[]{:S(2)}) async-start(), calls=%async_computation.4 | async-start | bytes 4718592 | tf_op jit(solution)/shard_map/reduce_scatter | solution.py:139
  35.1 2.3 %copy-start = (bf16[32,65536]{1,0:T(8,128)(2,1)S(1)}, bf16[32,65536]{1,0:T(8,128)(2,1)}, u32[]{:S(2)}) copy-start(bf16[32,65536]{1,0:T(8,128)(2,1)} %convolution_convert_fusion) | copy-start | bytes 12582916
  37.4 4.3 %copy-start.4 = (f32[128]{0:T(128)S(1)}, f32[128]{0:T(128)}, u32[]{:S(2)}) copy-start(f32[128]{0:T(128)} %param.9) | copy-start | bytes 1540
  37.7 1.9 copy-start.1
  39.7 2.8 %collective-permute-start = (bf16[1,8,128,512]{3,1,2,0:T(8,128)(2,1)S(1)}, bf16[1,8,128,512]{3,1,2,0:T(8,128)(2,1)}, u32[]{:S(2)}, u32[]{:S(2)}) collective-permute-start(bf16[1,8,128,512]{3,1,2,0:T(8,128)(2,1)S(1)} %get-tuple-element.16), channel_id=1, source_target_pairs={{0,1},{1,0},{2,3},{3,2},{4,5},{5,4},{6,7},{7,6},{8,9},{9,8},{10,11... | collective-permute-start | bytes 3145736 | tf_op jit(solution)/shard_map/ppermute | solution.py:19
  39.7 32.3 %collective-permute-start.1 = (bf16[1,8,128,512]{3,1,2,0:T(8,128)(2,1)S(1)}, bf16[1,8,128,512]{3,1,2,0:T(8,128)(2,1)}, u32[]{:S(2)}, u32[]{:S(2)}) collective-permute-start(bf16[1,8,128,512]{3,1,2,0:T(8,128)(2,1)S(1)} %get-tuple-element.15), channel_id=1, source_target_pairs={{0,2},{1,3},{2,0},{3,1},{4,6},{5,7},{6,4},{7,5},{8,10},{9,11},{10,... | collective-permute-start | bytes 3145736 | tf_op jit(solution)/shard_map/ppermute | solution.py:19
  39.7 54.5 %collective-permute-start.2 = (bf16[1,8,128,512]{3,1,2,0:T(8,128)(2,1)S(1)}, bf16[1,8,128,512]{3,1,2,0:T(8,128)(2,1)}, u32[]{:S(2)}, u32[]{:S(2)}) collective-permute-start(bf16[1,8,128,512]{3,1,2,0:T(8,128)(2,1)S(1)} %get-tuple-element.14), channel_id=1, source_target_pairs={{0,3},{1,2},{2,1},{3,0},{4,7},{5,6},{6,5},{7,4},{8,11},{9,10},{10,... | collective-permute-start | bytes 3145736 | tf_op jit(solution)/shard_map/ppermute | solution.py:19
  106.6 6.0 %copy-start.3 = (bf16[16,128]{1,0:T(8,128)(2,1)S(1)}, bf16[16,128]{1,0:T(8,128)(2,1)}, u32[]{:S(2)}) copy-start(bf16[16,128]{1,0:T(8,128)(2,1)} %param.8) | copy-start | bytes 12292
  133.2 4.2 %copy-start.2 = (bf16[48,32,512]{2,1,0:T(8,128)(2,1)S(1)}, bf16[48,32,512]{2,1,0:T(8,128)(2,1)}, u32[]{:S(2)}) copy-start(bf16[48,32,512]{2,1,0:T(8,128)(2,1)} %all-gather.2.cloned.1.call-done) | copy-start | bytes 4718596
Sparse Core Ops, SparseCore 0:
  28.6 63.2 reduce-scatter.6
  106.7 88.4 reduce-scatter.4
Sparse Core Ops, SparseCore 1:
  30.5 26.8 all-gather.1
